TPU v7x, 32 devices: a whole 2x2x4 slice. The times are simulated.
32 devices in a mesh: ep: 16 (over z, y, x), dp: 2 (over core).
Axes of the slice: x: 2, y: 2, z: 4, core: 2. Of those that a mesh axis runs over, the one named last changes fastest.
Arguments:
- tokens: bfloat16 [4096, 1024], P(('ep', 'dp')), may hold values from -6 to 6
- grad_out: bfloat16 [4096, 1024], P(('ep', 'dp')), may hold values from -3 to 3
- assign: int32 [4096, 2], P(('ep', 'dp')), may hold values from 0 to 15, as said below
- router_weight: bfloat16 [16, 1024], P('ep'), may hold values from -0.1875 to 0.1875
- w_gate: bfloat16 [16, 1024, 2048], P('ep', None, 'dp'), may hold values from -0.1875 to 0.1875
- w_up: bfloat16 [16, 1024, 2048], P('ep', None, 'dp'), may hold values from -0.1875 to 0.1875
- w_down: bfloat16 [16, 2048, 1024], P('ep', 'dp'), may hold values from -0.125 to 0.125
Outputs:
- grad_tokens: bfloat16 [4096, 1024], P(('ep', 'dp'))
- grad_router: float32 [16, 1024], P('ep')
- grad_gate: bfloat16 [16, 1024, 2048], P('ep', None, 'dp')
- grad_up: bfloat16 [16, 1024, 2048], P('ep', None, 'dp')
- grad_down: bfloat16 [16, 2048, 1024], P('ep', 'dp')
Inputs may be any that keep to these rules, and one draw needn't show every extreme that they name: `assign`: in each aligned block of 128 rows (the rows of one device) the two experts of a row differ and no expert is named by more than 24 entries; in every block one expert, the same for all blocks, is named by exactly 24 entries.
All inputs are finite; a program needn't handle non-finite values.
Results may differ from a plain program's by a relative error of at most 0.007.
Values may be sent and summed in bfloat16 or wider, within the bound.
A program may use at most 192 MiB of HBM per device.

v0:
```python
import jax
import jax.numpy as jnp
from jax import lax
from jax.sharding import PartitionSpec as P


def entry_slots(assign, experts, cap):
    flat = assign.reshape(-1)
    marks = (flat[:, None] == jnp.arange(experts, dtype=jnp.int32)[None, :]).astype(jnp.int32)
    before = jnp.cumsum(marks, axis=0) - marks
    ranks = jnp.sum(before * marks, axis=1)
    return flat * cap + ranks


def expert_grads(rows, upstream, gate_vals, wg, wu, wd):
    pre_a = jnp.dot(rows, wg, preferred_element_type=jnp.float32)
    pre_b = jnp.dot(rows, wu, preferred_element_type=jnp.float32)
    sigma = jax.nn.sigmoid(pre_a)
    active = pre_a * sigma
    hidden = (active * pre_b).astype(jnp.bfloat16)
    outer = jnp.dot(hidden, wd, preferred_element_type=jnp.float32)
    up_f = upstream.astype(jnp.float32)
    grad_gates = jnp.sum(up_f * outer, axis=1)
    scaled = (gate_vals.astype(jnp.float32)[:, None] * up_f).astype(jnp.bfloat16)
    grad_hidden = jnp.dot(scaled, wd.T, preferred_element_type=jnp.float32)
    grad_a = (grad_hidden * pre_b * sigma * (1.0 + pre_a * (1.0 - sigma))).astype(jnp.bfloat16)
    grad_b = (grad_hidden * active).astype(jnp.bfloat16)
    grad_rows = jnp.dot(grad_a, wg.T, preferred_element_type=jnp.float32) + jnp.dot(
        grad_b, wu.T, preferred_element_type=jnp.float32
    )
    g_gate = jnp.dot(rows.T, grad_a, preferred_element_type=jnp.float32)
    g_up = jnp.dot(rows.T, grad_b, preferred_element_type=jnp.float32)
    g_down = jnp.dot(hidden.T, scaled, preferred_element_type=jnp.float32)
    return (grad_rows, grad_gates, g_gate, g_up, g_down)


def local(tokens, grad_out, assign, router_weight, w_gate, w_up, w_down):
    tok_rows = tokens.shape[0]
    width = tokens.shape[1]
    router_full = lax.all_gather(router_weight, "ep", axis=0, tiled=True)
    experts = router_full.shape[0]
    cap = max(2, (3 * tok_rows + experts - 1) // experts)
    choose = (assign[:, :, None] == jnp.arange(experts, dtype=jnp.int32)[None, None, :]).astype(
        jnp.float32
    )
    scores = jnp.dot(tokens, router_full.T, preferred_element_type=jnp.float32)
    picked = jnp.sum(scores[:, None, :] * choose, axis=2)
    sig = jax.nn.sigmoid(picked)
    total = jnp.sum(sig, axis=1, keepdims=True)
    gates = sig / total
    slots = entry_slots(assign, experts, cap)
    entries = 2 * tok_rows
    table = (
        jnp.full((experts * cap,), -1, dtype=jnp.int32)
        .at[slots]
        .set(jnp.arange(entries, dtype=jnp.int32))
    )
    valid = table >= 0
    safe = jnp.maximum(table, 0)
    zero_low = jnp.zeros((), jnp.bfloat16)
    send_rows = jnp.where(valid[:, None], tokens[safe // 2], zero_low).reshape(experts, cap, width)
    send_ups = jnp.where(valid[:, None], grad_out[safe // 2], zero_low).reshape(experts, cap, width)
    send_gates = (
        jnp.where(valid, gates.reshape(-1)[safe], 0.0).astype(jnp.bfloat16).reshape(experts, cap)
    )
    got_rows, got_ups, got_gates = (
        lax.all_to_all(send_rows, "ep", split_axis=0, concat_axis=0, tiled=True),
        lax.all_to_all(send_ups, "ep", split_axis=0, concat_axis=0, tiled=True),
        lax.all_to_all(send_gates, "ep", split_axis=0, concat_axis=0, tiled=True),
    )
    rows = got_rows.reshape(experts * cap, width)
    ups = got_ups.reshape(experts * cap, width)
    gts = got_gates.reshape(experts * cap)
    both_rows, both_ups, both_gates = (
        lax.all_gather(rows, "dp", axis=0, tiled=True),
        lax.all_gather(ups, "dp", axis=0, tiled=True),
        lax.all_gather(gts, "dp", axis=0, tiled=True),
    )
    part_rows, part_gates, g_gate, g_up, g_down = expert_grads(
        both_rows, both_ups, both_gates, w_gate[0], w_up[0], w_down[0]
    )
    grad_rows, grad_gates = (
        lax.psum_scatter(part_rows, "dp", scatter_dimension=0, tiled=True),
        lax.psum_scatter(part_gates, "dp", scatter_dimension=0, tiled=True),
    )
    grad_gate = g_gate.astype(jnp.bfloat16)[None]
    grad_up = g_up.astype(jnp.bfloat16)[None]
    grad_down = g_down.astype(jnp.bfloat16)[None]
    back_rows, back_gates = (
        lax.all_to_all(
            grad_rows.astype(jnp.bfloat16).reshape(experts, cap, width),
            "ep",
            split_axis=0,
            concat_axis=0,
            tiled=True,
        ),
        lax.all_to_all(
            grad_gates.astype(jnp.bfloat16).reshape(experts, cap),
            "ep",
            split_axis=0,
            concat_axis=0,
            tiled=True,
        ),
    )
    entry_rows = (
        back_rows.reshape(experts * cap, width)[slots]
        .astype(jnp.float32)
        .reshape(tok_rows, 2, width)
    )
    entry_gates = back_gates.reshape(experts * cap)[slots].astype(jnp.float32).reshape(tok_rows, 2)
    mixed = jnp.sum(gates * entry_gates, axis=1, keepdims=True)
    grad_logit = (entry_gates - mixed) / total * sig * (1.0 - sig)
    dense = jnp.sum(grad_logit[:, :, None] * choose, axis=1)
    router_term = jnp.dot(dense, router_full.astype(jnp.float32), precision=lax.Precision.HIGHEST)
    grad_tokens = (jnp.sum(entry_rows, axis=1) + router_term).astype(jnp.bfloat16)
    partial_router = jnp.dot(dense.T, tokens.astype(jnp.float32), precision=lax.Precision.HIGHEST)
    summed = lax.psum(partial_router, ("ep", "dp"))
    grad_router = lax.dynamic_slice_in_dim(summed, lax.axis_index("ep"), 1, 0)
    return (grad_tokens, grad_router, grad_gate, grad_up, grad_down)


def solution(mesh):
    return jax.shard_map(
        local,
        mesh=mesh,
        in_specs=(
            P(("ep", "dp"), None),
            P(("ep", "dp"), None),
            P(("ep", "dp"), None),
            P("ep", None),
            P("ep", None, "dp"),
            P("ep", None, "dp"),
            P("ep", "dp", None),
        ),
        out_specs=(
            P(("ep", "dp"), None),
            P("ep", None),
            P("ep", None, "dp"),
            P("ep", None, "dp"),
            P("ep", "dp", None),
        ),
        check_vma=False,
    )
```

profile of v0, /device:TPU:1, one launch (start us, length us, event | category | flops | bytes accessed | tf_op | source)
XLA Modules:
  0.0 320.5 jit_solution(11369833928976403874)
XLA Ops:
  11.9 2.1 gather_fusion.1
  14.0 2.7 gather_fusion.2
  16.7 2.2 broadcast_select_fusion.1
  18.9 27.4 %all_to_all.35 = bf16[16,24,1024]{2,1,0:T(8,128)(2,1)} all-to-all(bf16[16,24,1024]{2,1,0:T(8,128)(2,1)S(1)} %get-tuple-element.14), channel_id=1, replica_groups=mesh['ep'=16,'dp'=2] {'ep'}, dimensions={0} | all-to-all | bytes 1572864 | tf_op jit(solution)/shard_map/all_to_all | solution.py:67
  46.4 4.1 %all-to-all-start.1 = ((bf16[16,24,1024]{2,1,0:T(8,128)(2,1)}), bf16[16,24,1024]{2,1,0:T(8,128)(2,1)S(1)}, u32[]{:S(2)}, u32[]{:S(2)}) async-start(bf16[16,24,1024]{2,1,0:T(8,128)(2,1)} %get-tuple-element.13), calls=%async_computation.1 | async-start | bytes 1572864 | tf_op jit(solution)/shard_map/all_to_all | solution.py:68
  50.5 39.2 %all-gather = bf16[16,1,1024]{2,1,0:T(2,128)(2,1)S(1)} all-gather(bf16[1,1,1024]{2,1,0:T(2,128)(2,1)S(1)} %bitcast.83), channel_id=1, replica_groups=mesh['ep'=16,'dp'=2] {'ep'}, dimensions={0}, use_global_device_ids=true | all-gather | bytes 34816 | tf_op jit(solution)/shard_map/all_gather | solution.py:40
  92.1 4.0 %fusion.5 = f32[768,1024]{1,0:T(8,128)S(1)} fusion(bf16[768,1024]{1,0:T(8,128)(2,1)} %all-gather.7.cloned.1.call-done, bf16[1,1024,1024]{2,1,0:T(8,128)(2,1)} %param.11), kind=kOutput, calls=%fused_computation.17 | convolution fusion | flops 1610612736 | bytes 6815744 | tf_op jit(solution)/shard_map/dot_general | solution.py:16
  96.1 1.7 copy-done.11
  97.8 4.2 %multiply_convert_fusion = (bf16[768,1024]{1,0:T(8,128)(2,1)}, f32[768,1024]{1,0:T(8,128)}) fusion(f32[768,1024]{1,0:T(8,128)S(1)} %fusion.5, bf16[768,1024]{1,0:T(8,128)(2,1)S(1)} %copy-done.7, bf16[1,1024,1024]{2,1,0:T(8,128)(2,1)S(1)} %copy-done), kind=kOutput, calls=%fused_computation.10 | convolution fusion | flops 1615331328 | bytes 11534336 | tf_op jit(solution)/shard_map/dot_general | solution.py:17
  102.0 4.8 %all-gather.5.cloned.1.call-done = bf16[768,1024]{1,0:T(8,128)(2,1)} async-done(((bf16[384,1024]{1,0:T(8,128)(2,1)}), bf16[768,1024]{1,0:T(8,128)(2,1)}) %all-gather.5.cloned.1.call-update) | async-done | bytes 1572880 | tf_op jit(solution)/shard_map/all_gather | solution.py:76
  106.8 4.4 %fusion.1 = f32[768]{0:T(1024)S(1)} fusion(bf16[768,1024]{1,0:T(8,128)(2,1)} %all-gather.5.cloned.1.call-done, bf16[768,1024]{1,0:T(8,128)(2,1)} %get-tuple-element.15, bf16[1,1024,1024]{2,1,0:T(8,128)(2,1)} %param.13), kind=kOutput, calls=%fused_computation.9 | convolution fusion | flops 1612971264 | bytes 5245952 | tf_op jit(solution)/shard_map/dot_general | solution.py:21
  111.1 6.0 %all-reduce = bf16[768]{0:T(1024)(128)(2,1)S(1)} all-reduce(f32[768]{0:T(1024)S(1)} %fusion.1), channel_id=3, replica_groups=mesh['ep'=16,'dp'=2] {'dp'}, use_global_device_ids=true, to_apply=%region_9.10.clone | all-reduce | flops 768 | bytes 4608
  117.9 3.5 %all-to-all-start.4 = ((bf16[16,1,24]{2,1,0:T(2,128)(2,1)}), bf16[16,1,24]{2,1,0:T(2,128)(2,1)S(1)}, u32[]{:S(2)}, u32[]{:S(2)}) async-start(bf16[16,1,24]{2,1,0:T(2,128)(2,1)} %all_to_all.29), calls=%async_computation.5 | async-start | bytes 16384 | tf_op jit(solution)/shard_map/all_to_all | solution.py:97
  121.5 6.0 %all-to-all-done.4 = bf16[16,1,24]{2,1,0:T(2,128)(2,1)S(1)} async-done(((bf16[16,1,24]{2,1,0:T(2,128)(2,1)}), bf16[16,1,24]{2,1,0:T(2,128)(2,1)S(1)}, u32[]{:S(2)}, u32[]{:S(2)}) %all-to-all-start.4) | async-done | bytes 800 | tf_op jit(solution)/shard_map/all_to_all | solution.py:97
  127.6 1.9 gather_fusion.4
  130.1 2.7 gather_fusion
  132.9 8.7 %all_to_all.36 = bf16[16,1,24]{2,1,0:T(2,128)(2,1)S(1)} all-to-all(bf16[16,1,24]{2,1,0:T(2,128)(2,1)S(1)} %all_to_all.28), channel_id=1, replica_groups=mesh['ep'=16,'dp'=2] {'ep'}, dimensions={0} | all-to-all | bytes 1536 | tf_op jit(solution)/shard_map/all_to_all | solution.py:69
  141.8 4.3 %all-gather.1 = bf16[2,1,384]{2,1,0:T(2,128)(2,1)S(1)} all-gather(bf16[1,1,384]{2,1,0:T(2,128)(2,1)S(1)} %reshape.229), channel_id=1, replica_groups=mesh['ep'=16,'dp'=2] {'dp'}, dimensions={0}, use_global_device_ids=true | all-gather | bytes 2304 | tf_op jit(solution)/shard_map/all_gather | solution.py:77
  146.1 6.8 %multiply_convert_fusion.1 = (bf16[768,1024]{1,0:T(8,128)(2,1)S(1)}, bf16[768,1024]{1,0:T(8,128)(2,1)S(1)}) fusion(f32[768,1024]{1,0:T(8,128)} %copy-done.11, f32[768,1024]{1,0:T(8,128)} %get-tuple-element.16, bf16[1,1024,1024]{2,1,0:T(8,128)(2,1)} %param.13, bf16[768,1024]{1,0:T(8,128)(2,1)} %all-gather.5.cloned.1.call-done, f32[768]{0:T(1024)S(1)} %reshape.231), kind=kOutput, calls=%fused_computation.11 | convolution fusion | flops 1623195648 | bytes 13110272 | tf_op jit(solution)/shard_map/dot_general | solution.py:25
  152.9 1.8 fusion.3
  154.8 3.5 %fusion.15 = f32[768,1024]{1,0:T(8,128)} fusion(f32[768,1024]{1,0:T(8,128)S(1)} %fusion.3, bf16[768,1024]{1,0:T(8,128)(2,1)S(1)} %get-tuple-element.9, bf16[1,1024,1024]{2,1,0:T(8,128)(2,1)S(1)} %copy-done), kind=kOutput, calls=%fused_computation.30 | convolution fusion | flops 1611399168 | bytes 9961472 | tf_op jit(solution)/shard_map/dot_general | solution.py:28
  158.4 7.8 %reduce-scatter.2.cloned.1.call-done = f32[384,1024]{1,0:T(8,128)} async-done(((f32[768,1024]{1,0:T(8,128)}), f32[384,1024]{1,0:T(8,128)}) %reduce-scatter.2.cloned.1.call-update) | async-done | bytes 1572880 | tf_op jit(solution)/shard_map/reduce_scatter | solution.py:83
  166.2 2.4 convert_element_type.75
  168.6 6.4 %all-to-all-start.3 = ((bf16[16,24,1024]{2,1,0:T(8,128)(2,1)}), bf16[16,24,1024]{2,1,0:T(8,128)(2,1)S(1)}, u32[]{:S(2)}, u32[]{:S(2)}) async-start(bf16[16,24,1024]{2,1,0:T(8,128)(2,1)} %bitcast.80), calls=%async_computation.4 | async-start | bytes 1572864 | tf_op jit(solution)/shard_map/all_to_all | solution.py:90
  176.2 5.2 %convert_bitcast_fusion.2 = bf16[1,1024,1024]{2,1,0:T(8,128)(2,1)} fusion(bf16[768,1024]{1,0:T(8,128)(2,1)} %all-gather.7.cloned.1.call-done, bf16[768,1024]{1,0:T(8,128)(2,1)} %copy-done.14), kind=kOutput, calls=%fused_computation.29 | convolution fusion | flops 1611661312 | bytes 5242880 | tf_op jit(solution)/shard_map/dot_general | solution.py:31
  181.4 3.3 %convert_bitcast_fusion = bf16[1,1024,1024]{2,1,0:T(8,128)(2,1)} fusion(bf16[768,1024]{1,0:T(8,128)(2,1)S(1)} %copy-done.15, bf16[768,1024]{1,0:T(8,128)(2,1)S(1)} %copy-done.9, f32[768]{0:T(1024)S(1)} %reshape.231), kind=kOutput, calls=%fused_computation.27 | convolution fusion | flops 1614020608 | bytes 5245952 | tf_op jit(solution)/shard_map/dot_general | solution.py:33
  184.7 3.2 convert_bitcast_fusion.1
  187.8 116.8 %all-reduce.3.cloned.1.call-done = f32[16,1024]{1,0:T(8,128)} async-done(((f32[16,1024]{1,0:T(8,128)}), f32[16,1024]{1,0:T(8,128)}) %all-reduce.3.cloned.1.call-update) | async-done | bytes 65552 | tf_op jit(solution)/shard_map/psum | solution.py:117
  306.0 2.0 gather_fusion.3
  308.0 1.7 reshape.174
  309.7 2.1 reduce_sum.69
  311.8 2.2 fusion.20
  (85 shorter events, 10.8 us)
Async XLA Ops:
  7.2 90.6 %copy-start = (bf16[1,1024,1024]{2,1,0:T(8,128)(2,1)S(1)}, bf16[1,1024,1024]{2,1,0:T(8,128)(2,1)}, u32[]{:S(2)}) copy-start(bf16[1,1024,1024]{2,1,0:T(8,128)(2,1)} %param.12) | copy-start | bytes 6291460
  7.2 4.7 %copy-start.2 = (bf16[128,1024]{1,0:T(8,128)(2,1)S(1)}, bf16[128,1024]{1,0:T(8,128)(2,1)}, u32[]{:S(2)}) copy-start(bf16[128,1024]{1,0:T(8,128)(2,1)} %param.8) | copy-start | bytes 786436
  7.2 84.9 %all-gather.7.cloned.1.call-start = ((), (), s32[]{:S(2)}) async-start(), calls=%async_computation.7 | async-start | bytes 2359296 | tf_op jit(solution)/shard_map/all_gather | solution.py:75
  11.9 2.1 copy-start.1
  18.9 31.7 %copy-start.5 = (bf16[1,1024]{1,0:T(2,128)(2,1)S(1)}, bf16[1,1024]{1,0:T(2,128)(2,1)}, u32[]{:S(2)}) copy-start(bf16[1,1024]{1,0:T(2,128)(2,1)} %param.10) | copy-start | bytes 6148
  46.3 44.5 %copy-start.4 = (s32[128,2]{0,1:T(2,128)S(1)}, s32[128,2]{0,1:T(2,128)}, u32[]{:S(2)}) copy-start(s32[128,2]{0,1:T(2,128)} %param.9) | copy-start | bytes 3076
  46.3 44.5 %copy-start.10 = (u32[32]{0:T(128)S(1)}, u32[32]{0:T(128)}, u32[]{:S(2)}) copy-start(u32[32]{0:T(128)} %constant.57) | copy-start | bytes 388
  46.4 43.5 %all-to-all-start.1 = ((bf16[16,24,1024]{2,1,0:T(8,128)(2,1)}), bf16[16,24,1024]{2,1,0:T(8,128)(2,1)S(1)}, u32[]{:S(2)}, u32[]{:S(2)}) async-start(bf16[16,24,1024]{2,1,0:T(8,128)(2,1)} %get-tuple-element.13), calls=%async_computation.1 | async-start | bytes 1572864 | tf_op jit(solution)/shard_map/all_to_all | solution.py:68
  50.5 56.3 %all-gather.5.cloned.1.call-start = ((), (), s32[]{:S(2)}) async-start(), calls=%async_computation.6 | async-start | bytes 2359296 | tf_op jit(solution)/shard_map/all_gather | solution.py:76
  89.9 0.9 copy-start.3
  92.1 5.7 %copy-start.7 = (bf16[768,1024]{1,0:T(8,128)(2,1)S(1)}, bf16[768,1024]{1,0:T(8,128)(2,1)}, u32[]{:S(2)}) copy-start(bf16[768,1024]{1,0:T(8,128)(2,1)} %all-gather.7.cloned.1.call-done) | copy-start | bytes 4718596
  96.1 1.7 copy-start.11
  117.9 9.5 %all-to-all-start.4 = ((bf16[16,1,24]{2,1,0:T(2,128)(2,1)}), bf16[16,1,24]{2,1,0:T(2,128)(2,1)S(1)}, u32[]{:S(2)}, u32[]{:S(2)}) async-start(bf16[16,1,24]{2,1,0:T(2,128)(2,1)} %all_to_all.29), calls=%async_computation.5 | async-start | bytes 16384 | tf_op jit(solution)/shard_map/all_to_all | solution.py:97
  121.4 44.8 %reduce-scatter.2.cloned.1.call-start = ((), (), s32[]{:S(2)}) async-start(), calls=%async_computation.8 | async-start | bytes 4718592 | tf_op jit(solution)/shard_map/reduce_scatter | solution.py:83
  146.1 6.8 %copy-start.6 = (bf16[1,1024,1024]{2,1,0:T(8,128)(2,1)S(1)}, bf16[1,1024,1024]{2,1,0:T(8,128)(2,1)}, u32[]{:S(2)}) copy-start(bf16[1,1024,1024]{2,1,0:T(8,128)(2,1)} %param.11) | copy-start | bytes 6291460
  152.9 1.9 copy-start.14
  152.9 1.9 copy-start.12
  168.6 137.4 %all-to-all-start.3 = ((bf16[16,24,1024]{2,1,0:T(8,128)(2,1)}), bf16[16,24,1024]{2,1,0:T(8,128)(2,1)S(1)}, u32[]{:S(2)}, u32[]{:S(2)}) async-start(bf16[16,24,1024]{2,1,0:T(8,128)(2,1)} %bitcast.80), calls=%async_computation.4 | async-start | bytes 1572864 | tf_op jit(solution)/shard_map/all_to_all | solution.py:90
  175.0 129.6 %all-reduce.3.cloned.1.call-start = ((), (), s32[]{:S(2)}) async-start(), calls=%async_computation.9 | async-start | bytes 131072 | tf_op jit(solution)/shard_map/psum | solution.py:117
  176.2 5.2 %copy-start.9 = (bf16[768,1024]{1,0:T(8,128)(2,1)S(1)}, bf16[768,1024]{1,0:T(8,128)(2,1)}, u32[]{:S(2)}) copy-start(bf16[768,1024]{1,0:T(8,128)(2,1)} %all-gather.5.cloned.1.call-done) | copy-start | bytes 4718596
  176.2 5.2 %copy-start.15 = (bf16[768,1024]{1,0:T(8,128)(2,1)S(1)}, bf16[768,1024]{1,0:T(8,128)(2,1)}, u32[]{:S(2)}) copy-start(bf16[768,1024]{1,0:T(8,128)(2,1)} %get-tuple-element.15) | copy-start | bytes 4718596
  181.4 3.3 %copy-start.8 = (bf16[768,1024]{1,0:T(8,128)(2,1)S(1)}, bf16[768,1024]{1,0:T(8,128)(2,1)}, u32[]{:S(2)}) copy-start(bf16[768,1024]{1,0:T(8,128)(2,1)} %all-gather.7.cloned.1.call-done) | copy-start | bytes 4718596
  181.4 3.3 %copy-start.13 = (bf16[768,1024]{1,0:T(8,128)(2,1)S(1)}, bf16[768,1024]{1,0:T(8,128)(2,1)}, u32[]{:S(2)}) copy-start(bf16[768,1024]{1,0:T(8,128)(2,1)} %copy-done.12) | copy-start | bytes 4718596
Sparse Core Ops, SparseCore 0:
  46.5 9.4 all-gather.6
  90.9 15.7 all-gather.4
  158.4 7.6 reduce-scatter.1
  181.7 122.9 all-reduce.2
where the time goes:
time: 321 us; the launch traced here: 320 us
  waiting for transfers between devices  135 us (42%)
  blocking collectives  85.7 us (27%)
  matrix products  39.5 us (12%)
  local copies, waits for them, and re-layouts  22.2 us (7%)
  between operations  14.8 us (5%)
  starting transfers between devices  14.4 us (4%)
  other arithmetic  8.53 us (3%)
    psum x1, waiting for transfers between devices, local(): summed = lax.psum(partial_router, ('ep', 'dp'))  117 us
    all_gather x1, blocking collectives, local(): router_full = lax.all_gather(router_weight, 'ep', axis=0, tiled=True)  39.2 us
    all_to_all x1, blocking collectives, local(): lax.all_to_all(send_rows, 'ep', split_axis=0, concat_axis=0, tiled=True)  27.4 us
    all_to_all x1, blocking collectives, local(): lax.all_to_all(send_gates, 'ep', split_axis=0, concat_axis=0, tiled=True)  8.73 us
    reduce_scatter x1, waiting for transfers between devices, local(): lax.psum_scatter(part_rows, 'dp', scatter_dimension=0, tiled=True)  7.8 us
    dot_general x1, matrix products, expert_grads(): grad_hidden = jnp.dot(scaled, wd.T, preferred_element_type=jnp.float32)  6.77 us
    all_to_all x1, starting transfers between devices, local(): lax.all_to_all(grad_rows.astype(jnp.bfloat16).reshape(experts, cap, width...  6.43 us
  transfers between devices with their start and end apart: 7, of which 4 were waited for; matrix products, arithmetic and copies ran while one was open for 7% of the time, Pallas kernels for 0%

commit v1 on v0

--- a/solution.py
+++ b/solution.py
@@ -114,7 +114,7 @@
     router_term = jnp.dot(dense, router_full.astype(jnp.float32), precision=lax.Precision.HIGHEST)
     grad_tokens = (jnp.sum(entry_rows, axis=1) + router_term).astype(jnp.bfloat16)
     partial_router = jnp.dot(dense.T, tokens.astype(jnp.float32), precision=lax.Precision.HIGHEST)
-    summed = lax.psum(partial_router, ("ep", "dp"))
+    summed = jnp.sum(lax.all_gather(partial_router, ("ep", "dp")), axis=0)
     grad_router = lax.dynamic_slice_in_dim(summed, lax.axis_index("ep"), 1, 0)
     return (grad_tokens, grad_router, grad_gate, grad_up, grad_down)
 

time: 321 us -> 247 us (0.77)
  waiting for transfers between devices: 135 us -> 60.4 us
    psum x1 -> x0, waiting for transfers between devices: 117 us -> none  [local(): summed = lax.psum(partial_router, ('ep', 'dp'))]
    all_gather x0 -> x1, waiting for transfers between devices: none -> 42.6 us  [local(): summed = jnp.sum(lax.all_gather(partial_router, ('ep', 'dp')), axis=0)]
  transfers between devices with their start and end apart: 7 -> 7, of which waited for: 4 -> 4; matrix products, arithmetic and copies ran while one was open for 7% -> 11% of each run, Pallas kernels for 0% -> 0%
where the time goes in v1:
time: 247 us; the launch traced here: 246 us
  blocking collectives  85.7 us (35%)
  waiting for transfers between devices  60.4 us (24%)
  matrix products  39.4 us (16%)
  local copies, waits for them, and re-layouts  21.4 us (9%)
  between operations  14.8 us (6%)
  starting transfers between devices  14.2 us (6%)
  other arithmetic  10.3 us (4%)
    all_gather x1, waiting for transfers between devices, local(): summed = jnp.sum(lax.all_gather(partial_router, ('ep', 'dp')), axis=0)  42.6 us
    all_gather x1, blocking collectives, local(): router_full = lax.all_gather(router_weight, 'ep', axis=0, tiled=True)  39.2 us
    all_to_all x1, blocking collectives, local(): lax.all_to_all(send_rows, 'ep', split_axis=0, concat_axis=0, tiled=True)  27.4 us
    all_to_all x1, blocking collectives, local(): lax.all_to_all(send_gates, 'ep', split_axis=0, concat_axis=0, tiled=True)  8.73 us
    reduce_scatter x1, waiting for transfers between devices, local(): lax.psum_scatter(part_rows, 'dp', scatter_dimension=0, tiled=True)  6.91 us
    dot_general x1, matrix products, expert_grads(): grad_hidden = jnp.dot(scaled, wd.T, preferred_element_type=jnp.float32)  6.74 us
    all_to_all x1, starting transfers between devices, local(): lax.all_to_all(grad_rows.astype(jnp.bfloat16).reshape(experts, cap, width...  6.44 us
    unnamed x1, blocking collectives  6.04 us
  transfers between devices with their start and end apart: 7, of which 4 were waited for; matrix products, arithmetic and copies ran while one was open for 11% of the time, Pallas kernels for 0%

profile of v1, /device:TPU:1, one launch (start us, length us, event | category | flops | bytes accessed | tf_op | source)
XLA Modules:
  0.0 246.1 jit_solution(10955125048628414096)
XLA Ops:
  11.9 2.1 gather_fusion.1
  14.0 2.7 %gather_fusion.2 = bf16[384,1024]{1,0:T(8,128)(2,1)} fusion(bf16[128,1024]{1,0:T(8,128)(2,1)S(1)} %copy-done.1, s32[1024]{0:T(1024)S(1)} %get-tuple-element.17), kind=kCustom, calls=%fused_computation.2 | custom fusion | bytes 1574400 | tf_op jit(solution)/shard_map/gather | solution.py:61
  16.7 2.2 broadcast_select_fusion.1
  18.9 27.4 %all_to_all.35 = bf16[16,24,1024]{2,1,0:T(8,128)(2,1)} all-to-all(bf16[16,24,1024]{2,1,0:T(8,128)(2,1)S(1)} %get-tuple-element.14), channel_id=1, replica_groups=mesh['ep'=16,'dp'=2] {'ep'}, dimensions={0} | all-to-all | bytes 1572864 | tf_op jit(solution)/shard_map/all_to_all | solution.py:67
  46.4 4.1 %all-to-all-start.1 = ((bf16[16,24,1024]{2,1,0:T(8,128)(2,1)}), bf16[16,24,1024]{2,1,0:T(8,128)(2,1)S(1)}, u32[]{:S(2)}, u32[]{:S(2)}) async-start(bf16[16,24,1024]{2,1,0:T(8,128)(2,1)} %get-tuple-element.13), calls=%async_computation.1 | async-start | bytes 1572864 | tf_op jit(solution)/shard_map/all_to_all | solution.py:68
  50.5 39.2 %all-gather.1 = bf16[16,1,1024]{2,1,0:T(2,128)(2,1)S(1)} all-gather(bf16[1,1,1024]{2,1,0:T(2,128)(2,1)S(1)} %bitcast.85), channel_id=1, replica_groups=mesh['ep'=16,'dp'=2] {'ep'}, dimensions={0}, use_global_device_ids=true | all-gather | bytes 34816 | tf_op jit(solution)/shard_map/all_gather | solution.py:40
  92.1 4.0 %fusion.5 = f32[768,1024]{1,0:T(8,128)S(1)} fusion(bf16[768,1024]{1,0:T(8,128)(2,1)} %all-gather.9.cloned.1.call-done, bf16[1,1024,1024]{2,1,0:T(8,128)(2,1)} %param.11), kind=kOutput, calls=%fused_computation.17 | convolution fusion | flops 1610612736 | bytes 6815744 | tf_op jit(solution)/shard_map/dot_general | solution.py:16
  97.8 4.2 %multiply_convert_fusion = (bf16[768,1024]{1,0:T(8,128)(2,1)}, f32[768,1024]{1,0:T(8,128)}) fusion(f32[768,1024]{1,0:T(8,128)S(1)} %fusion.5, bf16[768,1024]{1,0:T(8,128)(2,1)S(1)} %copy-done.7, bf16[1,1024,1024]{2,1,0:T(8,128)(2,1)S(1)} %copy-done), kind=kOutput, calls=%fused_computation.10 | convolution fusion | flops 1615331328 | bytes 11534336 | tf_op jit(solution)/shard_map/dot_general | solution.py:17
  102.0 4.7 %all-gather.7.cloned.1.call-done = bf16[768,1024]{1,0:T(8,128)(2,1)} async-done(((bf16[384,1024]{1,0:T(8,128)(2,1)}), bf16[768,1024]{1,0:T(8,128)(2,1)}) %all-gather.7.cloned.1.call-update) | async-done | bytes 1572880 | tf_op jit(solution)/shard_map/all_gather | solution.py:76
  106.8 4.4 %fusion.1 = f32[768]{0:T(1024)S(1)} fusion(bf16[768,1024]{1,0:T(8,128)(2,1)} %all-gather.7.cloned.1.call-done, bf16[768,1024]{1,0:T(8,128)(2,1)} %get-tuple-element.15, bf16[1,1024,1024]{2,1,0:T(8,128)(2,1)} %param.13), kind=kOutput, calls=%fused_computation.9 | convolution fusion | flops 1612971264 | bytes 5245952 | tf_op jit(solution)/shard_map/dot_general | solution.py:21
  111.1 6.0 %all-reduce = bf16[768]{0:T(1024)(128)(2,1)S(1)} all-reduce(f32[768]{0:T(1024)S(1)} %fusion.1), channel_id=4, replica_groups=mesh['ep'=16,'dp'=2] {'dp'}, use_global_device_ids=true, to_apply=%region_9.10.clone | all-reduce | flops 768 | bytes 4608
  118.0 3.5 %all-to-all-start.4 = ((bf16[16,1,24]{2,1,0:T(2,128)(2,1)}), bf16[16,1,24]{2,1,0:T(2,128)(2,1)S(1)}, u32[]{:S(2)}, u32[]{:S(2)}) async-start(bf16[16,1,24]{2,1,0:T(2,128)(2,1)} %all_to_all.29), calls=%async_computation.5 | async-start | bytes 16384 | tf_op jit(solution)/shard_map/all_to_all | solution.py:97
  121.5 6.0 %all-to-all-done.4 = bf16[16,1,24]{2,1,0:T(2,128)(2,1)S(1)} async-done(((bf16[16,1,24]{2,1,0:T(2,128)(2,1)}), bf16[16,1,24]{2,1,0:T(2,128)(2,1)S(1)}, u32[]{:S(2)}, u32[]{:S(2)}) %all-to-all-start.4) | async-done | bytes 800 | tf_op jit(solution)/shard_map/all_to_all | solution.py:97
  127.6 1.9 gather_fusion.4
  130.1 2.7 %gather_fusion = bf16[384]{0:T(512)(128)(2,1)S(1)} fusion(bf16[256]{0:T(256)(128)(2,1)S(1)} %reshape.173, s32[1024]{0:T(1024)S(1)} %get-tuple-element.18), kind=kCustom, calls=%fused_computation | custom fusion | bytes 3072 | tf_op jit(solution)/shard_map/gather | solution.py:64
  132.9 8.7 %all_to_all.36 = bf16[16,1,24]{2,1,0:T(2,128)(2,1)S(1)} all-to-all(bf16[16,1,24]{2,1,0:T(2,128)(2,1)S(1)} %all_to_all.28), channel_id=1, replica_groups=mesh['ep'=16,'dp'=2] {'ep'}, dimensions={0} | all-to-all | bytes 1536 | tf_op jit(solution)/shard_map/all_to_all | solution.py:69
  141.8 4.3 %all-gather.2 = bf16[2,1,384]{2,1,0:T(2,128)(2,1)S(1)} all-gather(bf16[1,1,384]{2,1,0:T(2,128)(2,1)S(1)} %reshape.230), channel_id=1, replica_groups=mesh['ep'=16,'dp'=2] {'dp'}, dimensions={0}, use_global_device_ids=true | all-gather | bytes 2304 | tf_op jit(solution)/shard_map/all_gather | solution.py:77
  146.1 6.7 %multiply_convert_fusion.1 = (bf16[768,1024]{1,0:T(8,128)(2,1)S(1)}, bf16[768,1024]{1,0:T(8,128)(2,1)S(1)}) fusion(f32[768,1024]{1,0:T(8,128)} %copy-done.11, f32[768,1024]{1,0:T(8,128)} %get-tuple-element.16, bf16[1,1024,1024]{2,1,0:T(8,128)(2,1)} %param.13, bf16[768,1024]{1,0:T(8,128)(2,1)} %all-gather.7.cloned.1.call-done, f32[768]{0:T(1024)S(1)} %reshape.232), kind=kOutput, calls=%fused_computation.11 | convolution fusion | flops 1623195648 | bytes 13110272 | tf_op jit(solution)/shard_map/dot_general | solution.py:25
  152.9 1.8 fusion.3
  154.8 3.5 %fusion.15 = f32[768,1024]{1,0:T(8,128)} fusion(f32[768,1024]{1,0:T(8,128)S(1)} %fusion.3, bf16[768,1024]{1,0:T(8,128)(2,1)S(1)} %get-tuple-element.9, bf16[1,1024,1024]{2,1,0:T(8,128)(2,1)S(1)} %copy-done), kind=kOutput, calls=%fused_computation.30 | convolution fusion | flops 1611399168 | bytes 9961472 | tf_op jit(solution)/shard_map/dot_general | solution.py:28
  159.2 6.9 %reduce-scatter.2.cloned.1.call-done = f32[384,1024]{1,0:T(8,128)} async-done(((f32[768,1024]{1,0:T(8,128)}), f32[384,1024]{1,0:T(8,128)}) %reduce-scatter.2.cloned.1.call-update) | async-done | bytes 1572880 | tf_op jit(solution)/shard_map/reduce_scatter | solution.py:83
  166.1 2.4 convert_element_type.75
  168.6 6.4 %all-to-all-start.3 = ((bf16[16,24,1024]{2,1,0:T(8,128)(2,1)}), bf16[16,24,1024]{2,1,0:T(8,128)(2,1)S(1)}, u32[]{:S(2)}, u32[]{:S(2)}) async-start(bf16[16,24,1024]{2,1,0:T(8,128)(2,1)} %bitcast.81), calls=%async_computation.4 | async-start | bytes 1572864 | tf_op jit(solution)/shard_map/all_to_all | solution.py:90
  175.0 5.2 %convert_bitcast_fusion.2 = bf16[1,1024,1024]{2,1,0:T(8,128)(2,1)} fusion(bf16[768,1024]{1,0:T(8,128)(2,1)} %all-gather.9.cloned.1.call-done, bf16[768,1024]{1,0:T(8,128)(2,1)} %copy-done.14), kind=kOutput, calls=%fused_computation.29 | convolution fusion | flops 1611661312 | bytes 5242880 | tf_op jit(solution)/shard_map/dot_general | solution.py:31
  180.3 3.2 %convert_bitcast_fusion.1 = bf16[1,1024,1024]{2,1,0:T(8,128)(2,1)} fusion(bf16[768,1024]{1,0:T(8,128)(2,1)S(1)} %copy-done.8, bf16[768,1024]{1,0:T(8,128)(2,1)S(1)} %copy-done.13), kind=kOutput, calls=%fused_computation.28 | convolution fusion | flops 1611661312 | bytes 5242880 | tf_op jit(solution)/shard_map/dot_general | solution.py:32
  183.4 3.3 %convert_bitcast_fusion = bf16[1,1024,1024]{2,1,0:T(8,128)(2,1)} fusion(bf16[768,1024]{1,0:T(8,128)(2,1)S(1)} %copy-done.15, bf16[768,1024]{1,0:T(8,128)(2,1)S(1)} %copy-done.9, f32[768]{0:T(1024)S(1)} %reshape.232), kind=kOutput, calls=%fused_computation.27 | convolution fusion | flops 1614020608 | bytes 5245952 | tf_op jit(solution)/shard_map/dot_general | solution.py:33
  186.7 42.6 %all-gather.11.cloned.1.call-done = f32[512,1024]{1,0:T(8,128)} async-done(((f32[16,1024]{1,0:T(8,128)}), f32[512,1024]{1,0:T(8,128)}) %all-gather.11.cloned.1.call-update) | async-done | bytes 2097168 | tf_op jit(solution)/shard_map/all_gather | solution.py:117
  229.3 1.7 reduce_sum.82
  231.7 2.0 gather_fusion.3
  233.6 1.7 reshape.174
  235.3 2.1 reduce_sum.78
  237.4 2.2 fusion.20
  (86 shorter events, 11.5 us)
Async XLA Ops:
  7.2 90.7 %copy-start = (bf16[1,1024,1024]{2,1,0:T(8,128)(2,1)S(1)}, bf16[1,1024,1024]{2,1,0:T(8,128)(2,1)}, u32[]{:S(2)}) copy-start(bf16[1,1024,1024]{2,1,0:T(8,128)(2,1)} %param.12) | copy-start | bytes 6291460
  7.2 4.7 %copy-start.2 = (bf16[128,1024]{1,0:T(8,128)(2,1)S(1)}, bf16[128,1024]{1,0:T(8,128)(2,1)}, u32[]{:S(2)}) copy-start(bf16[128,1024]{1,0:T(8,128)(2,1)} %param.8) | copy-start | bytes 786436
  7.2 84.9 %all-gather.9.cloned.1.call-start = ((), (), s32[]{:S(2)}) async-start(), calls=%async_computation.7 | async-start | bytes 2359296 | tf_op jit(solution)/shard_map/all_gather | solution.py:75
  11.9 2.1 copy-start.1
  18.9 31.7 %copy-start.5 = (bf16[1,1024]{1,0:T(2,128)(2,1)S(1)}, bf16[1,1024]{1,0:T(2,128)(2,1)}, u32[]{:S(2)}) copy-start(bf16[1,1024]{1,0:T(2,128)(2,1)} %param.10) | copy-start | bytes 6148
  46.3 44.5 %copy-start.4 = (s32[128,2]{0,1:T(2,128)S(1)}, s32[128,2]{0,1:T(2,128)}, u32[]{:S(2)}) copy-start(s32[128,2]{0,1:T(2,128)} %param.9) | copy-start | bytes 3076
  46.3 44.5 %copy-start.10 = (u32[32]{0:T(128)S(1)}, u32[32]{0:T(128)}, u32[]{:S(2)}) copy-start(u32[32]{0:T(128)} %constant.57) | copy-start | bytes 388
  46.4 43.5 %all-to-all-start.1 = ((bf16[16,24,1024]{2,1,0:T(8,128)(2,1)}), bf16[16,24,1024]{2,1,0:T(8,128)(2,1)S(1)}, u32[]{:S(2)}, u32[]{:S(2)}) async-start(bf16[16,24,1024]{2,1,0:T(8,128)(2,1)} %get-tuple-element.13), calls=%async_computation.1 | async-start | bytes 1572864 | tf_op jit(solution)/shard_map/all_to_all | solution.py:68
  50.5 56.3 %all-gather.7.cloned.1.call-start = ((), (), s32[]{:S(2)}) async-start(), calls=%async_computation.6 | async-start | bytes 2359296 | tf_op jit(solution)/shard_map/all_gather | solution.py:76
  89.9 0.9 copy-start.3
  92.1 5.7 %copy-start.7 = (bf16[768,1024]{1,0:T(8,128)(2,1)S(1)}, bf16[768,1024]{1,0:T(8,128)(2,1)}, u32[]{:S(2)}) copy-start(bf16[768,1024]{1,0:T(8,128)(2,1)} %all-gather.9.cloned.1.call-done) | copy-start | bytes 4718596
  96.1 1.7 copy-start.11
  118.0 9.5 %all-to-all-start.4 = ((bf16[16,1,24]{2,1,0:T(2,128)(2,1)}), bf16[16,1,24]{2,1,0:T(2,128)(2,1)S(1)}, u32[]{:S(2)}, u32[]{:S(2)}) async-start(bf16[16,1,24]{2,1,0:T(2,128)(2,1)} %all_to_all.29), calls=%async_computation.5 | async-start | bytes 16384 | tf_op jit(solution)/shard_map/all_to_all | solution.py:97
  121.4 44.7 %reduce-scatter.2.cloned.1.call-start = ((), (), s32[]{:S(2)}) async-start(), calls=%async_computation.8 | async-start | bytes 4718592 | tf_op jit(solution)/shard_map/reduce_scatter | solution.py:83
  146.1 6.8 %copy-start.6 = (bf16[1,1024,1024]{2,1,0:T(8,128)(2,1)S(1)}, bf16[1,1024,1024]{2,1,0:T(8,128)(2,1)}, u32[]{:S(2)}) copy-start(bf16[1,1024,1024]{2,1,0:T(8,128)(2,1)} %param.11) | copy-start | bytes 6291460
  152.9 1.9 copy-start.14
  152.9 1.9 copy-start.12
  158.3 71.1 %all-gather.11.cloned.1.call-start = ((), (), s32[]{:S(2)}) async-start(), calls=%async_computation.9 | async-start | bytes 2162688 | tf_op jit(solution)/shard_map/all_gather | solution.py:117
  168.6 63.1 %all-to-all-start.3 = ((bf16[16,24,1024]{2,1,0:T(8,128)(2,1)}), bf16[16,24,1024]{2,1,0:T(8,128)(2,1)S(1)}, u32[]{:S(2)}, u32[]{:S(2)}) async-start(bf16[16,24,1024]{2,1,0:T(8,128)(2,1)} %bitcast.81), calls=%async_computation.4 | async-start | bytes 1572864 | tf_op jit(solution)/shard_map/all_to_all | solution.py:90
  175.0 5.2 %copy-start.8 = (bf16[768,1024]{1,0:T(8,128)(2,1)S(1)}, bf16[768,1024]{1,0:T(8,128)(2,1)}, u32[]{:S(2)}) copy-start(bf16[768,1024]{1,0:T(8,128)(2,1)} %all-gather.9.cloned.1.call-done) | copy-start | bytes 4718596
  175.0 5.2 %copy-start.13 = (bf16[768,1024]{1,0:T(8,128)(2,1)S(1)}, bf16[768,1024]{1,0:T(8,128)(2,1)}, u32[]{:S(2)}) copy-start(bf16[768,1024]{1,0:T(8,128)(2,1)} %copy-done.12) | copy-start | bytes 4718596
  180.2 3.2 %copy-start.9 = (bf16[768,1024]{1,0:T(8,128)(2,1)S(1)}, bf16[768,1024]{1,0:T(8,128)(2,1)}, u32[]{:S(2)}) copy-start(bf16[768,1024]{1,0:T(8,128)(2,1)} %all-gather.7.cloned.1.call-done) | copy-start | bytes 4718596
  180.2 3.2 %copy-start.15 = (bf16[768,1024]{1,0:T(8,128)(2,1)S(1)}, bf16[768,1024]{1,0:T(8,128)(2,1)}, u32[]{:S(2)}) copy-start(bf16[768,1024]{1,0:T(8,128)(2,1)} %get-tuple-element.15) | copy-start | bytes 4718596
Sparse Core Ops, SparseCore 0:
  46.5 9.4 all-gather.8
  90.9 15.7 all-gather.6
  158.4 7.6 reduce-scatter.1
  169.4 59.8 all-gather.10
